TPU v7x, 128 devices: a whole 4x4x4 slice. The times are simulated.
128 devices in a mesh: band: 4 (over y), patch: 32 (over x, z, core).
Axes of the slice: x: 4, y: 4, z: 4, core: 2. Of those that a mesh axis runs over, the one named last changes fastest.
Arguments:
- images: float32 [4, 1024, 168, 168], P('band', 'patch'), may hold values from -48 to 48
- coeffs: bfloat16 [4, 1024, 3, 128, 128], P('band', 'patch'), may hold values from 0.29882812 to 1.5
- inverse_var: float32 [4, 1024, 128, 128], P('band', 'patch'), may hold values from 0.3 to 3
- bad_lines: int32 [4, 1024, 2], P('band', 'patch'), may hold values from 0 to 127
- destinations: int32 [4, 1024, 1], P('band', 'patch'), may hold values from 0 to 31; in each aligned block of 32 rows (0 to 31, 32 to 63, ..., all dimensions but the last counted through in order) at most 2 rows name the same one
- tile_slots: int32 [4, 1024], P('band', 'patch'), may hold values from 0 to 15
Outputs:
- coadd: float32 [4, 32, 256, 1024], P('band', 'patch')
- detection: float32 [32, 256, 1024], P('patch', 'band')
Inputs may be any that keep to these rules, and one draw needn't show every extreme that they name: `destinations`: among the 32 pieces of one band held by one index of patch (aligned blocks), no patch is named more than 2 times, a bound that some block reaches.
All inputs are finite; a program needn't handle non-finite values.
Results may differ from a plain program's by a relative error of at most 0.00035.
Values sent between devices are 32-bit elements; how exact they have to be, the bound alone decides.
No kernel may reach another device: no remote copies, remote signals or barrier semaphores. Data moves between devices by JAX's collectives and lax.ppermute only.
A program may use at most 192 MiB of HBM per device.

v0:
```python
import jax
import jax.numpy as jnp
from jax import lax
from jax.sharding import PartitionSpec as P

TILES_X = 8
TILES_Y = 2


HIGHEST = lax.Precision.HIGHEST
FRACTIONS = (0.12, 0.25, 0.45)
FLOOR = 0.5


def kernel_bands(tile_side, half_taps):
    offset = (
        jnp.arange(tile_side + 2 * half_taps, dtype=jnp.int32)[None, :]
        - jnp.arange(tile_side, dtype=jnp.int32)[:, None]
    )
    inside = (offset >= 0) & (offset <= 2 * half_taps)
    centred = (offset - half_taps).astype(jnp.float32)
    tap_offsets = (jnp.arange(2 * half_taps + 1, dtype=jnp.int32) - half_taps).astype(jnp.float32)
    matrices = []
    for fraction in FRACTIONS:
        sigma_width = fraction * half_taps
        tap_total = jnp.sum(jnp.exp(-0.5 * (tap_offsets / sigma_width) ** 2))
        matrices.append(
            jnp.where(inside, jnp.exp(-0.5 * (centred / sigma_width) ** 2) / tap_total, 0.0)
        )
    return jnp.stack(matrices)


def match_pieces(images, coeffs, bands):
    rows_done = jnp.einsum("kyi,pij->pkyj", bands, images, precision=HIGHEST)
    smoothed = jnp.einsum("pkyj,kxj->pkyx", rows_done, bands, precision=HIGHEST)
    return jnp.sum(coeffs * smoothed, axis=1)


def slot_matrix(targets, tile_index, owners_count, slot_depth):
    owners = jnp.arange(owners_count, dtype=jnp.int32)
    onehot = (targets[:, None] == owners[None, :]).astype(jnp.int32)
    before = jnp.cumsum(onehot, axis=0) - onehot
    slot_rank = jnp.sum(before * onehot, axis=1)
    slot_index = targets * slot_depth + slot_rank
    slot_range = jnp.arange(owners_count * slot_depth, dtype=jnp.int32)
    chosen = slot_range[:, None] == slot_index[None, :]
    selector = chosen.astype(jnp.float32)
    position = jnp.sum(jnp.where(chosen, tile_index[None, :] + 1, 0), axis=1) - 1
    return (selector, position.astype(jnp.float32).reshape(owners_count, slot_depth))


def pack_slots(selector, slot_data, owners_count, slot_depth):
    flat_rows = slot_data.reshape(slot_data.shape[0], -1)
    packed = jnp.dot(selector, flat_rows, precision=HIGHEST, preferred_element_type=jnp.float32)
    return packed.reshape((owners_count, slot_depth) + slot_data.shape[1:])


def per_device(images, coeffs, inverse_var, bad_lines, destinations, tile_slots):
    owners_count = lax.axis_size("patch")
    piece_count = images.shape[1]
    slot_depth = max(2, 2 * piece_count // owners_count)
    tile_side = inverse_var.shape[-1]
    half_taps = (images.shape[-1] - tile_side) // 2
    bands = kernel_bands(tile_side, half_taps)
    line_index = jnp.arange(tile_side, dtype=jnp.int32)
    lines = bad_lines[0]
    keep_pixel = (line_index[None, :, None] != lines[:, 0][:, None, None]) & (
        line_index[None, None, :] != lines[:, 1][:, None, None]
    )
    weight = jnp.where(keep_pixel, inverse_var[0], 0.0)
    selector, position = slot_matrix(destinations[0, :, 0], tile_slots[0], owners_count, slot_depth)
    raw_slots = pack_slots(selector, images[0], owners_count, slot_depth)
    coeff_slots = pack_slots(selector, coeffs[0].astype(jnp.float32), owners_count, slot_depth)
    weight_slots = pack_slots(selector, weight, owners_count, slot_depth)
    image_part = lax.all_to_all(raw_slots, "patch", split_axis=0, concat_axis=0, tiled=True)
    coeff_part = lax.all_to_all(coeff_slots, "patch", split_axis=0, concat_axis=0, tiled=True)
    weight_part = lax.all_to_all(weight_slots, "patch", split_axis=0, concat_axis=0, tiled=True)
    place_part = lax.all_to_all(position, "patch", split_axis=0, concat_axis=0, tiled=True)
    lead_shape = image_part.shape[:2]
    matched = match_pieces(
        image_part.reshape((-1,) + image_part.shape[2:]),
        coeff_part.reshape((-1,) + coeff_part.shape[2:]),
        bands,
    )
    matched = matched.reshape(lead_shape + (tile_side, tile_side))
    numer_slots = weight_part * matched
    flat_places = place_part.reshape(-1)
    tile_targets = jnp.arange(TILES_Y * TILES_X, dtype=jnp.float32)
    spread = (tile_targets[:, None] == flat_places[None, :]).astype(jnp.float32)

    def assemble(planes):
        summed = jnp.dot(
            spread,
            planes.reshape(flat_places.shape[0], -1),
            precision=HIGHEST,
            preferred_element_type=jnp.float32,
        )
        return (
            summed.reshape(TILES_Y, TILES_X, tile_side, tile_side)
            .transpose(0, 2, 1, 3)
            .reshape(TILES_Y * tile_side, TILES_X * tile_side)
        )

    numerator = assemble(numer_slots)
    denominator = assemble(weight_part)
    coadd = numerator / jnp.maximum(denominator, FLOOR)
    detection = lax.psum_scatter(numerator * coadd, "band", scatter_dimension=0, tiled=True)
    return (coadd[None, None], detection[None])


def solution(mesh):
    in_specs = (
        P("band", "patch", None, None),
        P("band", "patch", None, None, None),
        P("band", "patch", None, None),
        P("band", "patch", None),
        P("band", "patch", None),
        P("band", "patch"),
    )
    out_specs = (P("band", "patch", None, None), P("patch", "band", None))
    return jax.shard_map(
        per_device, mesh=mesh, in_specs=in_specs, out_specs=out_specs, check_vma=False
    )
```

profile of v0, /device:TPU:1, one launch (start us, length us, event | category | flops | bytes accessed | tf_op | source)
XLA Modules:
  0.0 570.5 jit_solution(14553900260620366143)
XLA Ops:
  7.2 0.7 fusion.30
  7.9 0.1 reduce_window_sum.11
  7.9 0.8 select_reduce_fusion.1
  8.8 0.7 multiply_add_fusion.2
  9.4 0.7 add_bitcast_fusion
  10.1 0.1 select_reduce_fusion
  10.2 0.7 convert_element_type.51
  10.9 9.4 %all-to-all-start = ((f32[32,1,2]{2,1,0:T(1,128)}), f32[32,1,2]{2,1,0:T(1,128)S(1)}, u32[]{:S(2)}, u32[]{:S(2)}) async-start(f32[32,1,2]{2,1,0:T(1,128)} %bitcast.2), calls=%async_computation | async-start | bytes 32768 | tf_op jit(solution)/shard_map/all_to_all | solution.py:78
  20.4 6.0 %reshape_squeeze.3 = f32[32,28224]{1,0:T(8,128)} reshape(f32[1,32,168,168]{3,2,1,0:T(8,128)} %param.6) | data formatting | bytes 7225344 | tf_op jit(solution)/shard_map/reshape;squeeze | solution.py:53
  26.4 7.0 %dot_general.48 = f32[168,168,32]{1,0,2:T(8,128)} reshape(f32[28224,32]{0,1:T(8,128)} %bitcast.153) | data formatting | bytes 7225344 | tf_op jit(solution)/shard_map/dot_general | solution.py:54
  33.3 8.0 %fusion.3 = f32[32,2,168,168]{3,0,2,1:T(8,128)S(1)} fusion(f32[168,168,32]{1,0,2:T(8,128)} %dot_general.48, s32[32]{0:T(128)S(1)} %multiply_add_fusion.2, s32[32,2]{0,1:T(2,128)S(1)} %multiply_add_fusion), kind=kOutput, calls=%fused_computation.4 | convolution fusion | flops 693635072 | bytes 10838400 | tf_op jit(solution)/shard_map/dot_general | solution.py:54
  41.4 10.4 %copy.37 = f32[32,2,168,168]{3,2,1,0:T(8,128)} copy(f32[32,2,168,168]{3,0,2,1:T(8,128)S(1)} %fusion.3) | data formatting | bytes 14450688 | tf_op jit(solution)/shard_map/dot_general | solution.py:54
  51.8 0.0 all-to-all-done
  51.8 7.4 %all-to-all-start.3 = ((f32[32,2,168,168]{3,2,1,0:T(8,128)}), f32[32,2,168,168]{3,2,1,0:T(8,128)}, u32[]{:S(2)}, u32[]{:S(2)}) async-start(f32[32,2,168,168]{3,2,1,0:T(8,128)} %copy.37), calls=%async_computation.3 | async-start | bytes 22020096 | tf_op jit(solution)/shard_map/all_to_all | solution.py:75
  59.2 3.4 reshape.316
  62.6 0.7 copy.54
  63.3 6.7 %fusion.12 = f32[32,2,3,128,128]{4,0,3,2,1:T(8,128)} fusion(bf16[3,128,128,32]{2,1,0,3:T(8,128)(2,1)S(1)} %bitcast.155, s32[32]{0:T(128)S(1)} %multiply_add_fusion.2, s32[32,2]{0,1:T(2,128)S(1)} %multiply_add_fusion), kind=kOutput, calls=%fused_computation.15 | convolution fusion | flops 201328640 | bytes 15729024 | tf_op jit(solution)/shard_map/dot_general | solution.py:54
  70.0 16.4 %copy.35 = f32[32,2,3,128,128]{4,3,2,1,0:T(8,128)} copy(f32[32,2,3,128,128]{4,0,3,2,1:T(8,128)} %fusion.12) | data formatting | bytes 25165824 | tf_op jit(solution)/shard_map/dot_general | solution.py:54
  86.4 0.0 copy-start.1
  86.4 0.0 copy-start
  86.4 125.2 %all-to-all-done.3 = f32[32,2,168,168]{3,2,1,0:T(8,128)} async-done(((f32[32,2,168,168]{3,2,1,0:T(8,128)}), f32[32,2,168,168]{3,2,1,0:T(8,128)}, u32[]{:S(2)}, u32[]{:S(2)}) %all-to-all-start.3) | async-done | bytes 7225376 | tf_op jit(solution)/shard_map/all_to_all | solution.py:75
  211.6 34.8 %all-to-all-start.2 = ((f32[32,2,3,128,128]{4,3,2,1,0:T(8,128)}), f32[32,2,3,128,128]{4,3,2,1,0:T(8,128)}, u32[]{:S(2)}, u32[]{:S(2)}) async-start(f32[32,2,3,128,128]{4,3,2,1,0:T(8,128)} %copy.35), calls=%async_computation.2 | async-start | bytes 25165824 | tf_op jit(solution)/shard_map/all_to_all | solution.py:76
  246.4 0.0 copy-done.1
  246.4 0.1 iota_compare_fusion
  246.5 0.7 broadcast_and_fusion
  247.2 0.0 copy-done
  247.2 3.6 fusion.16
  250.9 4.4 copy.33
  255.2 164.7 %all-to-all-done.2 = f32[32,2,3,128,128]{4,3,2,1,0:T(8,128)} async-done(((f32[32,2,3,128,128]{4,3,2,1,0:T(8,128)}), f32[32,2,3,128,128]{4,3,2,1,0:T(8,128)}, u32[]{:S(2)}, u32[]{:S(2)}) %all-to-all-start.2) | async-done | bytes 12582944 | tf_op jit(solution)/shard_map/all_to_all | solution.py:76
  419.9 31.0 %all-to-all-start.1 = ((f32[32,2,128,128]{3,2,1,0:T(8,128)}), f32[32,2,128,128]{3,2,1,0:T(8,128)}, u32[]{:S(2)}, u32[]{:S(2)}) async-start(f32[32,2,128,128]{3,2,1,0:T(8,128)} %copy.33), calls=%async_computation.1 | async-start | bytes 8388608 | tf_op jit(solution)/shard_map/all_to_all | solution.py:77
  450.9 0.0 reduce-scatter.2.cloned.1.call-start
  451.0 0.6 exponential_reduce_fusion
  451.6 0.6 exponential_reduce_fusion.1
  452.2 0.6 exponential_reduce_fusion.2
  452.8 0.6 divide_select_fusion.2
  453.5 1.4 divide_select_fusion
  454.8 0.5 broadcast.317
  455.3 0.7 reduce.3
  456.0 0.1 eq.85
  456.1 26.9 %fusion.19 = f32[64,168,3,128]{3,1,0,2:T(8,128)} fusion(f32[64,168,168,1]{2,1,0,3:T(8,128)} %bitcast.23, f32[1,128,168]{1,2,0:T(8,128)S(1)} %get-tuple-element.8, f32[1,128,168]{1,2,0:T(8,128)S(1)} %get-tuple-element.9, f32[1,128,168]{1,2,0:T(8,128)S(1)} %divide_select_fusion.2), kind=kOutput, calls=%fused_computation.28 | convolution fusion | flops 8323725312 | bytes 23998464 | tf_op jit(solution)/shard_map/kyi,pij->pkyj/dot_general | solution.py:34
  483.1 12.6 %copy.39 = f32[64,3,128,128]{2,3,0,1:T(8,128)} copy(f32[64,3,128,128]{3,2,1,0:T(8,128)} %bitcast.16) | data formatting | bytes 25165824 | tf_op jit(solution)/shard_map/reshape | solution.py:82
  495.6 23.3 %fusion.2 = f32[64,128,128]{1,2,0:T(8,128)} fusion(f32[64,3,128,128]{2,3,0,1:T(8,128)} %copy.39, f32[64,168,3,128]{3,1,0,2:T(8,128)} %fusion.19, f32[1,128,168]{1,2,0:T(8,128)S(1)} %get-tuple-element.8, f32[1,128,168]{1,2,0:T(8,128)S(1)} %get-tuple-element.9, f32[1,128,168]{1,2,0:T(8,128)S(1)} %divide_select_fusion.2), kind=kOutput, calls=%fused_computation.3 | convolution fusion | flops 6347159552 | bytes 33550336 | tf_op jit(solution)/shard_map/pkyj,kxj->pkyx/dot_general | solution.py:35
  518.9 5.8 %copy.40 = f32[64,128,128]{2,1,0:T(8,128)} copy(f32[64,128,128]{1,2,0:T(8,128)} %fusion.2) | data formatting | bytes 8388608 | tf_op jit(solution)/shard_map/reduce_sum | solution.py:36
  524.8 0.0 all-to-all-done.1
  524.8 4.2 mul.71
  529.0 3.9 fusion.10
  532.8 5.9 %bitcast_divide_fusion = (f32[2,128,8,128]{3,2,1,0:T(8,128)S(1)}, f32[2,8,128,128]{3,1,2,0:T(8,128)S(1)}) fusion(f32[2,8,128,128]{3,1,2,0:T(8,128)S(1)} %fusion.10, f32[64]{0:T(128)S(1)} %eq.85, f32[2,8]{1,0:T(2,128)S(1)} %multiply_add_fusion.1, f32[8,8,128,128]{3,2,1,0:T(8,128)} %bitcast.61), kind=kOutput, calls=%fused_computation.25 | convolution fusion | flops 201851904 | bytes 7340352 | tf_op jit(solution)/shard_map/dot_general | solution.py:92
  538.7 1.4 divide_multiply_fusion
  540.2 0.0 reduce-scatter.2.cloned.1.call-update
  540.2 1.1 div.109
  541.3 21.9 %reduce-scatter.2.cloned.1.call-done = f32[64,1024]{1,0:T(8,128)} async-done(((f32[256,1024]{1,0:T(8,128)}), f32[64,1024]{1,0:T(8,128)}) %reduce-scatter.2.cloned.1.call-update) | async-done | bytes 262160 | tf_op jit(solution)/shard_map/reduce_scatter | solution.py:107
  (4 shorter events, 0.0 us)
Async XLA Ops:
  10.9 40.8 %all-to-all-start = ((f32[32,1,2]{2,1,0:T(1,128)}), f32[32,1,2]{2,1,0:T(1,128)S(1)}, u32[]{:S(2)}, u32[]{:S(2)}) async-start(f32[32,1,2]{2,1,0:T(1,128)} %bitcast.2), calls=%async_computation | async-start | bytes 32768 | tf_op jit(solution)/shard_map/all_to_all | solution.py:78
  51.8 159.8 %all-to-all-start.3 = ((f32[32,2,168,168]{3,2,1,0:T(8,128)}), f32[32,2,168,168]{3,2,1,0:T(8,128)}, u32[]{:S(2)}, u32[]{:S(2)}) async-start(f32[32,2,168,168]{3,2,1,0:T(8,128)} %copy.37), calls=%async_computation.3 | async-start | bytes 22020096 | tf_op jit(solution)/shard_map/all_to_all | solution.py:75
  86.4 160.0 %copy-start.1 = (s32[1,32,2]{1,2,0:T(2,128)S(1)}, s32[1,32,2]{1,2,0:T(2,128)}, u32[]{:S(2)}) copy-start(s32[1,32,2]{1,2,0:T(2,128)} %param.9) | copy-start | bytes 772
  86.4 160.8 %copy-start = (f32[1,32,128,128]{3,2,1,0:T(8,128)S(1)}, f32[1,32,128,128]{3,2,1,0:T(8,128)}, u32[]{:S(2)}) copy-start(f32[1,32,128,128]{3,2,1,0:T(8,128)} %param.8) | copy-start | bytes 6291460
  211.6 208.3 %all-to-all-start.2 = ((f32[32,2,3,128,128]{4,3,2,1,0:T(8,128)}), f32[32,2,3,128,128]{4,3,2,1,0:T(8,128)}, u32[]{:S(2)}, u32[]{:S(2)}) async-start(f32[32,2,3,128,128]{4,3,2,1,0:T(8,128)} %copy.35), calls=%async_computation.2 | async-start | bytes 25165824 | tf_op jit(solution)/shard_map/all_to_all | solution.py:76
  419.9 104.8 %all-to-all-start.1 = ((f32[32,2,128,128]{3,2,1,0:T(8,128)}), f32[32,2,128,128]{3,2,1,0:T(8,128)}, u32[]{:S(2)}, u32[]{:S(2)}) async-start(f32[32,2,128,128]{3,2,1,0:T(8,128)} %copy.33), calls=%async_computation.1 | async-start | bytes 8388608 | tf_op jit(solution)/shard_map/all_to_all | solution.py:77
  450.9 112.3 %reduce-scatter.2.cloned.1.call-start = ((), (), s32[]{:S(2)}) async-start(), calls=%async_computation.5 | async-start | bytes 1310720 | tf_op jit(solution)/shard_map/reduce_scatter | solution.py:107
Sparse Core Ops, SparseCore 0:
  540.3 22.8 reduce-scatter.1
where the time goes:
time: 581 us; the launch traced here: 571 us
  waiting for transfers between devices  312 us (54%)
  starting transfers between devices  82.7 us (14%)
  matrix products  78.3 us (13%)
  local copies, waits for them, and re-layouts  69.1 us (12%)
  between operations  14.6 us (3%)
  other arithmetic  14 us (2%)
    all_to_all x1, waiting for transfers between devices, per_device(): lax.all_to_all(coeff_slots, 'patch', split_axis=0, concat_axis=0, tiled=T...  165 us
    all_to_all x1, waiting for transfers between devices, per_device(): lax.all_to_all(raw_slots, 'patch', split_axis=0, concat_axis=0, tiled=True)  125 us
    dot_general x4, local copies, waits for them, and re-layouts, pack_slots(): jnp.dot(selector, flat_rows, precision=HIGHEST, preferred_element_type=jn...  38.1 us
    all_to_all x1, starting transfers between devices, per_device(): lax.all_to_all(coeff_slots, 'patch', split_axis=0, concat_axis=0, tiled=T...  34.8 us
    all_to_all x1, starting transfers between devices, per_device(): lax.all_to_all(weight_slots, 'patch', split_axis=0, concat_axis=0, tiled=...  31 us
    dot_general x1, matrix products, match_pieces(): rows_done = jnp.einsum('kyi,pij->pkyj', bands, images, precision=HIGHEST)  26.9 us
    dot_general x1, matrix products, match_pieces(): smoothed = jnp.einsum('pkyj,kxj->pkyx', rows_done, bands, precision=HIGHEST)  23.3 us
    reduce_scatter x1, waiting for transfers between devices, per_device(): lax.psum_scatter(numerator * coadd, 'band', scatter_dimension=0, tiled=True)  21.9 us
  transfers between devices with their start and end apart: 5, of which 3 were waited for; matrix products, arithmetic and copies ran while one was open for 25% of the time, Pallas kernels for 0%

commit v1 on v0

v1 whole, which is shorter than its diff:
```python
import jax
import jax.numpy as jnp
import ml_dtypes
import numpy as np
from jax import lax
from jax.experimental import pallas as pl
from jax.experimental.pallas import tpu as pltpu
from jax.sharding import PartitionSpec as P

TILES_X = 8
TILES_Y = 2
TILES = TILES_X * TILES_Y
FRACTIONS = (0.12, 0.25, 0.45)
KERNELS = len(FRACTIONS)
FLOOR = 0.5
EVERY = ("band", "patch")
GROUP = 8
LANES = 128
VMEM_LIMIT = 60 << 20
PLACE_LIMIT = 24 << 20


def split_pair(values):
    high = values.astype(jnp.bfloat16)
    low = (values - high.astype(jnp.float32)).astype(jnp.bfloat16)
    return high, low


def kernel_bands(side, taps):
    offset = np.arange(side + 2 * taps)[None, :] - np.arange(side)[:, None]
    inside = (offset >= 0) & (offset <= 2 * taps)
    reach = np.arange(2 * taps + 1) - taps
    pairs = []
    for fraction in FRACTIONS:
        width = fraction * taps
        total = np.exp(-0.5 * (reach / width) ** 2).sum()
        full = np.where(inside, np.exp(-0.5 * ((offset - taps) / width) ** 2) / total, 0.0)
        full = full.astype(np.float32)
        high = full.astype(ml_dtypes.bfloat16)
        low = (full - high.astype(np.float32)).astype(ml_dtypes.bfloat16)
        pairs.append((high, low))
    columns = np.concatenate([h.T for h, _ in pairs] + [l.T for _, l in pairs], axis=1)
    rows = np.stack([np.concatenate(pair, axis=0) for pair in pairs])
    return columns, rows


def match_body(lines, image_ref, coeff_ref, inverse_ref, columns_ref, rows_ref, out_ref, scratch):
    side = inverse_ref.shape[-1]
    half = side // 2
    group = pl.program_id(0)
    row_index = lax.broadcasted_iota(jnp.int32, (side, side), 0)
    lane_index = lax.broadcasted_iota(jnp.int32, (side, side), 1)
    left = lax.broadcasted_iota(jnp.int32, (8, side), 1) < half
    flat = scratch

    def one_piece(p, carry):
        high, low = split_pair(image_ref[p])
        first = jnp.dot(high, columns_ref[...], preferred_element_type=jnp.float32)
        second = jnp.dot(low, columns_ref[:, : KERNELS * side], preferred_element_type=jnp.float32)
        across = first[:, : KERNELS * side] + (first[:, KERNELS * side :] + second)
        matched = None
        for k in range(KERNELS):
            part = jnp.concatenate(split_pair(across[:, k * side : (k + 1) * side]), axis=1)
            both = jnp.dot(rows_ref[k], part, preferred_element_type=jnp.float32)
            smooth = both[:side, :side] + (both[:side, side:] + both[side:, :side])
            term = coeff_ref[p, k].astype(jnp.float32) * smooth
            matched = term if matched is None else matched + term
        piece = group * GROUP + p
        masked = (row_index == lines[0, piece]) | (lane_index == lines[1, piece])
        weight = jnp.where(masked, 0.0, inverse_ref[p])
        for plane, values in enumerate((weight * matched, weight)):
            for v in range(half // 8):
                upper = values[8 * v : 8 * v + 8]
                lower = values[half + 8 * v : half + 8 * v + 8]
                swapped_lower = pltpu.roll(lower, half, 1)
                swapped_upper = pltpu.roll(upper, half, 1)
                start = 8 * v * 32 + plane * 8 + p
                flat[pl.ds(start, 8, stride=32), :] = jnp.where(left, upper, swapped_lower)
                flat[pl.ds(start + 16, 8, stride=32), :] = jnp.where(left, swapped_upper, lower)
        return carry

    lax.fori_loop(0, GROUP, one_piece, 0, unroll=8)
    out_ref[...] = flat[...].reshape(out_ref.shape)


def match_pieces(images, coeffs, inverse_var, lines, slabs):
    pieces, wide = images.shape[0], images.shape[-1]
    side = inverse_var.shape[-1]
    columns, rows = kernel_bands(side, (wide - side) // 2)
    return pl.pallas_call(
        match_body,
        grid_spec=pltpu.PrefetchScalarGridSpec(
            num_scalar_prefetch=1,
            grid=(pieces // GROUP,),
            in_specs=[
                pl.BlockSpec((GROUP, wide, wide), lambda g, s: (g, 0, 0)),
                pl.BlockSpec((GROUP, KERNELS, side, side), lambda g, s: (g, 0, 0, 0)),
                pl.BlockSpec((GROUP, side, side), lambda g, s: (g, 0, 0)),
                pl.BlockSpec(columns.shape, lambda g, s: (0, 0)),
                pl.BlockSpec(rows.shape, lambda g, s: (0, 0, 0)),
            ],
            out_specs=pl.BlockSpec((slabs, 2 * GROUP, LANES), lambda g, s: (0, g, 0)),
            scratch_shapes=[pltpu.VMEM((slabs * 2 * GROUP, LANES), jnp.float32)],
        ),
        out_shape=jax.ShapeDtypeStruct((slabs, 2 * pieces, LANES), jnp.float32),
        compiler_params=pltpu.CompilerParams(vmem_limit_bytes=VMEM_LIMIT),
        name="match_pieces",
    )(lines, images, coeffs, inverse_var, jnp.asarray(columns), jnp.asarray(rows))


def sum_body(codes_ref, slab_ref, out_ref, total_ref):
    band = pl.program_id(0)
    holders, depth, lanes = slab_ref.shape
    patches = out_ref.shape[0] // pl.num_programs(0)
    pieces = holders * depth // 2
    both = slab_ref[...].reshape(holders * depth // (2 * GROUP), 2 * GROUP, lanes)
    values = jnp.concatenate(
        [both[:, :GROUP].reshape(pieces, lanes), both[:, GROUP:].reshape(pieces, lanes)], axis=1
    )
    high, low = split_pair(values)
    bins = lax.broadcasted_iota(jnp.int32, (patches * TILES, lanes), 0)
    joined = holders * lanes // pieces
    chosen = []
    for row in range(0, holders, joined):
        code = jnp.sum(codes_ref[0, row : row + joined, :], axis=0, keepdims=True)
        chosen.append(jnp.where(bins == code, 1.0, 0.0).astype(jnp.bfloat16))
    chosen = jnp.concatenate(chosen, axis=1)
    sums = jnp.dot(chosen, high, preferred_element_type=jnp.float32) + jnp.dot(
        chosen, low, preferred_element_type=jnp.float32
    )
    numerator, denominator = sums[:, :lanes], sums[:, lanes:]
    coadd = numerator / jnp.maximum(denominator, FLOOR)
    out_ref[pl.ds(band * patches, patches), :TILES, :] = coadd.reshape(patches, TILES, lanes)
    term = numerator * coadd

    @pl.when(band == 0)
    def _():
        total_ref[...] = term

    @pl.when(band > 0)
    def _():
        total_ref[...] += term

    @pl.when(band == pl.num_programs(0) - 1)
    def _():
        total = total_ref[...].reshape(patches, TILES_Y, TILES_X, lanes)
        for target in range(4):
            out_ref[target * patches : (target + 1) * patches, TILES:, :] = total[:, target // 2]


def sum_slabs(codes, slabs, bands, patches):
    devices, depth, lanes = slabs.shape
    rows = TILES + TILES_X
    return pl.pallas_call(
        sum_body,
        grid=(bands,),
        in_specs=[
            pl.BlockSpec((1, *codes.shape[1:]), lambda b: (b, 0, 0)),
            pl.BlockSpec((devices // bands, depth, lanes), lambda b: (b, 0, 0)),
        ],
        out_specs=pl.BlockSpec((devices, rows, lanes), lambda b: (0, 0, 0)),
        out_shape=jax.ShapeDtypeStruct((devices, rows, lanes), jnp.float32),
        scratch_shapes=[pltpu.VMEM((patches * TILES, lanes), jnp.float32)],
        compiler_params=pltpu.CompilerParams(vmem_limit_bytes=VMEM_LIMIT),
        name="sum_slabs",
    )(codes, slabs)


def place_body(which, part_ref, coadd_ref, detection_ref):
    lanes = part_ref.shape[-1]
    half = lanes // 2
    rows = TILES + TILES_X
    left = lax.broadcasted_iota(jnp.int32, (8, lanes), 1) < half
    for row in range(0, coadd_ref.shape[1], 8):
        for tile in range(rows):
            even = part_ref[pl.ds(2 * row * rows + tile, 8, stride=2 * rows), :]
            odd = part_ref[pl.ds((2 * row + 1) * rows + tile, 8, stride=2 * rows), :]
            upper = jnp.where(left, even, pltpu.roll(odd, half, 1))
            lower = jnp.where(left, pltpu.roll(even, half, 1), odd)
            column = (tile % TILES_X) * lanes
            if tile < TILES:
                top = 2 * (tile // TILES_X)
                coadd_ref[top, row : row + 8, column : column + lanes] = upper
                coadd_ref[top + 1, row : row + 8, column : column + lanes] = lower
            else:
                detection_ref[row : row + 8, column : column + lanes] = jnp.where(
                    which[0] == 0, upper, lower
                )


def place_parts(which, parts, side):
    devices, rows, lanes = parts.shape
    steps = 4
    half = side // 2
    return pl.pallas_call(
        place_body,
        grid_spec=pltpu.PrefetchScalarGridSpec(
            num_scalar_prefetch=1,
            grid=(steps,),
            in_specs=[pl.BlockSpec((devices * rows // steps, lanes), lambda g, s: (g, 0))],
            out_specs=[
                pl.BlockSpec((2 * TILES_Y, half // steps, TILES_X * lanes), lambda g, s: (0, g, 0)),
                pl.BlockSpec((half // steps, TILES_X * lanes), lambda g, s: (g, 0)),
            ],
        ),
        out_shape=[
            jax.ShapeDtypeStruct((2 * TILES_Y, half, TILES_X * lanes), jnp.float32),
            jax.ShapeDtypeStruct((half, TILES_X * lanes), jnp.float32),
        ],
        compiler_params=pltpu.CompilerParams(vmem_limit_bytes=PLACE_LIMIT),
        name="place_parts",
    )(which, parts.reshape(devices * rows, lanes))


def per_device(images, coeffs, inverse_var, bad_lines, destinations, tile_slots):
    bands, patches = lax.axis_size("band"), lax.axis_size("patch")
    side = inverse_var.shape[-1]
    code = destinations[0, :, 0] * TILES + tile_slots[0]
    pieces = code.shape[0]
    here = (jnp.arange(LANES) // pieces) == lax.axis_index("patch") % (LANES // pieces)
    code = jnp.where(here, jnp.tile(code, LANES // pieces), 0)
    code = jnp.broadcast_to(code, (bands * patches, 1, LANES))
    codes = lax.all_to_all(code, EVERY, split_axis=0, concat_axis=0, tiled=True)
    slabs = match_pieces(images[0], coeffs[0], inverse_var[0], bad_lines[0].T, bands * patches)
    slabs = lax.all_to_all(slabs, EVERY, split_axis=0, concat_axis=0, tiled=True)
    parts = sum_slabs(codes.reshape(bands, patches, LANES), slabs, bands, patches)
    parts = lax.all_to_all(parts, EVERY, split_axis=0, concat_axis=0, tiled=True)
    which = jnp.full((1,), lax.axis_index("band") % 2, jnp.int32)
    coadd, detection = place_parts(which, parts, side)
    return (coadd.reshape(1, 1, TILES_Y * side, TILES_X * side), detection[None])


def solution(mesh):
    in_specs = (
        P("band", "patch", None, None),
        P("band", "patch", None, None, None),
        P("band", "patch", None, None),
        P("band", "patch", None),
        P("band", "patch", None),
        P("band", "patch"),
    )
    out_specs = (P("band", "patch", None, None), P("patch", "band", None))
    return jax.shard_map(
        per_device, mesh=mesh, in_specs=in_specs, out_specs=out_specs, check_vma=False
    )
```

time: 581 us -> 133 us (0.23); the launches traced: 571 us -> 133 us
  waiting for transfers between devices: 312 us -> 24.8 us
  matrix products: 78.3 us -> 0 us
  local copies, waits for them, and re-layouts: 69.1 us -> 0.76 us
  starting transfers between devices: 82.7 us -> 16 us
  blocking collectives: 0 us -> 62.9 us
  Pallas kernels: 0 us -> 26.8 us
  between operations: 14.6 us -> 0.68 us
  other arithmetic: 14 us -> 0.68 us
    all_to_all x4 -> x2, waiting for transfers between devices: 290 us -> 24.8 us  [the longest x1 24.8 us: per_device(): lax.all_to_all(parts, EVERY, split_axis=0, concat_axis=0, tiled=True)]
    dot_general x7 -> x0, matrix products: 78.3 us -> none  [the longest x1 26.9 us: match_pieces(): rows_done = jnp.einsum('kyi,pij->pkyj', bands, images, precision=HIGHEST)]
    all_to_all x4 -> x2, starting transfers between devices: 82.7 us -> 16 us  [the longest x1 11.5 us: per_device(): codes = lax.all_to_all(code, EVERY, split_axis=0, concat_axis=0, tiled=True)]
    all_to_all x0 -> x1, blocking collectives: none -> 62.9 us  [per_device(): lax.all_to_all(slabs, EVERY, split_axis=0, concat_axis=0, tiled=True)]
    dot_general x4 -> x0, local copies, waits for them, and re-layouts: 38.1 us -> none  [pack_slots(): jnp.dot(selector, flat_rows, precision=HIGHEST, preferred_element_type=jn...]
    pallas_call x0 -> x3, Pallas kernels: none -> 26.8 us  [the longest x1 18.8 us: match_pieces(): pl.pallas_call(match_body, grid_spec=pltpu.PrefetchScalarGridSpec(num_sca...]
    reduce_scatter x1 -> x0, waiting for transfers between devices: 21.9 us -> none  [per_device(): lax.psum_scatter(numerator * coadd, 'band', scatter_dimension=0, tiled=True)]
    reshape x2 -> x0, local copies, waits for them, and re-layouts: 15.9 us -> none  [the longest x1 12.6 us: per_device(): coeff_part.reshape((-1,) + coeff_part.shape[2:])]
  transfers between devices with their start and end apart: 5 -> 2, of which waited for: 3 -> 1; matrix products, arithmetic and copies ran while one was open for 25% -> 0% of each run, Pallas kernels for 0% -> 14%
where the time goes in v1:
time: 133 us
  blocking collectives  62.9 us (47%)
  Pallas kernels  26.8 us (20%)
  waiting for transfers between devices  24.8 us (19%)
  starting transfers between devices  16 us (12%)
    all_to_all x1, blocking collectives, per_device(): lax.all_to_all(slabs, EVERY, split_axis=0, concat_axis=0, tiled=True)  62.9 us
    all_to_all x1, waiting for transfers between devices, per_device(): lax.all_to_all(parts, EVERY, split_axis=0, concat_axis=0, tiled=True)  24.8 us
    pallas_call x1, Pallas kernels, match_pieces(): pl.pallas_call(match_body, grid_spec=pltpu.PrefetchScalarGridSpec(num_sca...  18.8 us
    all_to_all x1, starting transfers between devices, per_device(): codes = lax.all_to_all(code, EVERY, split_axis=0, concat_axis=0, tiled=True)  11.5 us
    pallas_call x1, Pallas kernels, sum_slabs(): pl.pallas_call(sum_body, grid=(bands,), in_specs=[pl.BlockSpec((1, *codes...  6.05 us
    all_to_all x1, starting transfers between devices, per_device(): lax.all_to_all(parts, EVERY, split_axis=0, concat_axis=0, tiled=True)  4.5 us
  transfers between devices with their start and end apart: 2, of which 1 were waited for; matrix products, arithmetic and copies ran while one was open for 0% of the time, Pallas kernels for 14%

profile of v1, /device:TPU:1, one launch (start us, length us, event | category | flops | bytes accessed | tf_op | source)
XLA Modules:
  0.0 132.6 jit_solution(14975711836968579407)
XLA Ops:
  0.6 0.7 fusion
  1.3 0.1 tile.13
  1.4 0.7 broadcast_in_dim.12
  2.1 11.5 %all-to-all-start = ((s32[128,1,128]{2,1,0:T(1,128)}), s32[128,1,128]{2,1,0:T(1,128)S(1)}, u32[]{:S(2)}, u32[]{:S(2)}) async-start(s32[128,1,128]{2,1,0:T(1,128)} %broadcast_in_dim.12), calls=%async_computation | async-start | bytes 131072 | tf_op jit(solution)/shard_map/all_to_all | solution.py:223
  13.6 18.8 %match_pieces.1 = f32[128,64,128]{2,1,0:T(8,128)} custom-call(s32[2,32]{1,0:T(2,128)} %bitcast.22, f32[32,168,168]{2,1,0:T(8,128)} %bitcast.18, bf16[32,3,128,128]{3,2,1,0:T(8,128)(2,1)} %bitcast.19, f32[32,128,128]{2,1,0:T(8,128)} %bitcast.20, bf16[168,768]{1,0:T(8,128)(2,1)} %constant.55.clone.columns_ref, bf16[3,256,168]{2,1,0:T(8,128)(2,1)} %constant.56.clone.rows_ref), custom_call_target="tpu_custom_call" | custom-call | tf_op jit(solution)/shard_map/match_pieces/pallas_call | solution.py:90
  32.4 0.0 all-to-all-done
  32.4 0.0 copy-start
  32.4 62.9 %all_to_all.15.slab_ref = f32[128,64,128]{2,1,0:T(8,128)} all-to-all(f32[128,64,128]{2,1,0:T(8,128)} %match_pieces.1), channel_id=1, replica_groups=mesh['band'=4,'patch'=32] {'band','patch'}, dimensions={0} | all-to-all | bytes 8388608 | tf_op jit(solution)/shard_map/all_to_all | solution.py:225
  95.2 0.0 copy-done
  95.2 6.0 %sum_slabs.1 = f32[128,24,128]{2,1,0:T(8,128)} custom-call(s32[4,32,128]{2,1,0:T(8,128)} %bitcast.21, f32[128,64,128]{2,1,0:T(8,128)} %all_to_all.15.slab_ref), custom_call_target="tpu_custom_call" | custom-call | tf_op jit(solution)/shard_map/sum_slabs/pallas_call | solution.py:154
  101.3 4.5 %all-to-all-start.2 = ((f32[128,24,128]{2,1,0:T(8,128)}), f32[128,24,128]{2,1,0:T(8,128)S(1)}, u32[]{:S(2)}, u32[]{:S(2)}) async-start(f32[128,24,128]{2,1,0:T(8,128)} %sum_slabs.1), calls=%async_computation.2 | async-start | bytes 3145728 | tf_op jit(solution)/shard_map/all_to_all | solution.py:227
  105.8 24.8 %all-to-all-done.2 = f32[128,24,128]{2,1,0:T(8,128)S(1)} async-done(((f32[128,24,128]{2,1,0:T(8,128)}), f32[128,24,128]{2,1,0:T(8,128)S(1)}, u32[]{:S(2)}, u32[]{:S(2)}) %all-to-all-start.2) | async-done | bytes 1572896 | tf_op jit(solution)/shard_map/all_to_all | solution.py:227
  130.6 2.0 %place_parts.1 = (f32[4,64,1024]{2,1,0:T(8,128)}, f32[64,1024]{1,0:T(8,128)}) custom-call(s32[1]{0:T(128)} %bitcast.which, f32[3072,128]{1,0:T(8,128)S(1)} %bitcast.17), custom_call_target="tpu_custom_call" | custom-call | tf_op jit(solution)/shard_map/place_parts/pallas_call | solution.py:195
  (2 shorter events, 0.0 us)
Async XLA Ops:
  2.1 30.3 %all-to-all-start = ((s32[128,1,128]{2,1,0:T(1,128)}), s32[128,1,128]{2,1,0:T(1,128)S(1)}, u32[]{:S(2)}, u32[]{:S(2)}) async-start(s32[128,1,128]{2,1,0:T(1,128)} %broadcast_in_dim.12), calls=%async_computation | async-start | bytes 131072 | tf_op jit(solution)/shard_map/all_to_all | solution.py:223
  32.4 62.9 %copy-start = (s32[128,1,128]{2,1,0:T(1,128)}, s32[128,1,128]{2,1,0:T(1,128)S(1)}, u32[]{:S(2)}) copy-start(s32[128,1,128]{2,1,0:T(1,128)S(1)} %all-to-all-done) | copy-start | bytes 196612
  101.3 29.3 %all-to-all-start.2 = ((f32[128,24,128]{2,1,0:T(8,128)}), f32[128,24,128]{2,1,0:T(8,128)S(1)}, u32[]{:S(2)}, u32[]{:S(2)}) async-start(f32[128,24,128]{2,1,0:T(8,128)} %sum_slabs.1), calls=%async_computation.2 | async-start | bytes 3145728 | tf_op jit(solution)/shard_map/all_to_all | solution.py:227

commit v2 on v1

v2 whole, which is shorter than its diff:
```python
import functools

import jax
import jax.numpy as jnp
import ml_dtypes
import numpy as np
from jax import lax
from jax.experimental import pallas as pl
from jax.experimental.pallas import tpu as pltpu
from jax.sharding import PartitionSpec as P

TILES_X = 8
TILES_Y = 2
TILES = TILES_X * TILES_Y
FRACTIONS = (0.12, 0.25, 0.45)
KERNELS = len(FRACTIONS)
FLOOR = 0.5
EVERY = ("band", "patch")
GROUP = 4
LANES = 128
VMEM_LIMIT = 60 << 20
SMALL_LIMIT = 24 << 20


def split_pair(values):
    high = values.astype(jnp.bfloat16)
    low = (values - high.astype(jnp.float32)).astype(jnp.bfloat16)
    return high, low


def kernel_bands(side, taps):
    offset = np.arange(side + 2 * taps)[None, :] - np.arange(side)[:, None]
    inside = (offset >= 0) & (offset <= 2 * taps)
    reach = np.arange(2 * taps + 1) - taps
    stacked = []
    for fraction in FRACTIONS:
        width = fraction * taps
        total = np.exp(-0.5 * (reach / width) ** 2).sum()
        full = np.where(inside, np.exp(-0.5 * ((offset - taps) / width) ** 2) / total, 0.0)
        full = full.astype(np.float32)
        high = full.astype(ml_dtypes.bfloat16)
        low = (full - high.astype(np.float32)).astype(ml_dtypes.bfloat16)
        stacked.append(np.concatenate([high, low, high], axis=1))
    columns = np.concatenate([matrix.T for matrix in stacked], axis=1)
    rows = np.stack(stacked)
    return columns, rows


def cut_rows(flat, values, start, step):
    side = values.shape[-1]
    half = side // 2
    left = lax.broadcasted_iota(jnp.int32, (8, side), 1) < half
    for row in range(0, half, 8):
        upper = values[row : row + 8]
        lower = values[half + row : half + row + 8]
        first = jnp.where(left, upper, pltpu.roll(lower, half, 1))
        second = jnp.where(left, pltpu.roll(upper, half, 1), lower)
        flat[pl.ds(start + 2 * row * step, 8, stride=2 * step), :] = first
        flat[pl.ds(start + (2 * row + 1) * step, 8, stride=2 * step), :] = second


def weight_of(lines, inverse, piece):
    row_index = lax.broadcasted_iota(jnp.int32, inverse.shape, 0)
    lane_index = lax.broadcasted_iota(jnp.int32, inverse.shape, 1)
    masked = (row_index == lines[0, piece]) | (lane_index == lines[1, piece])
    return jnp.where(masked, 0.0, inverse)


def match_body(lines, code_ref, image_ref, coeff_ref, inverse_ref, columns_ref, rows_ref, out_ref, *, depth):
    side = inverse_ref.shape[-1]
    group = pl.program_id(0)
    pieces = depth // 2

    @pl.when(group == 0)
    def _():
        code = jnp.broadcast_to(code_ref[...], (8, code_ref.shape[-1]))
        for slab in range(0, out_ref.shape[0] // depth, 8):
            out_ref[pl.ds(slab * depth + depth - 1, 8, stride=depth), :] = code

    def one_pair(pair, carry):
        across = []
        for p in (2 * pair, 2 * pair + 1):
            high, low = split_pair(image_ref[p])
            stacked = jnp.concatenate([high, high, low], axis=1)
            across.append(jnp.dot(stacked, columns_ref[...], preferred_element_type=jnp.float32))
        matched = None
        for k in range(KERNELS):
            both = jnp.concatenate([part[:, k * side : (k + 1) * side] for part in across], axis=1)
            high = both.astype(jnp.bfloat16).astype(jnp.float32)
            stacked = jnp.concatenate([high, high, both - high], axis=0).astype(jnp.bfloat16)
            smooth = jnp.dot(rows_ref[k], stacked, preferred_element_type=jnp.float32)
            terms = [
                coeff_ref[2 * pair + n, k].astype(jnp.float32) * smooth[:, n * side : (n + 1) * side]
                for n in range(2)
            ]
            matched = terms if matched is None else [a + b for a, b in zip(matched, terms)]
        for n in range(2):
            p = 2 * pair + n
            piece = group * GROUP + p
            weight = weight_of(lines, inverse_ref[p], piece)
            cut_rows(out_ref, weight * matched[n], piece, depth)
            cut_rows(out_ref, weight, pieces + piece, depth)
        return carry

    lax.fori_loop(0, GROUP // 2, one_pair, 0, unroll=True)


def match_pieces(images, coeffs, inverse_var, lines, code, slabs):
    pieces, wide = images.shape[0], images.shape[-1]
    side = inverse_var.shape[-1]
    depth = 2 * pieces + 1
    columns, rows = kernel_bands(side, (wide - side) // 2)
    return pl.pallas_call(
        functools.partial(match_body, depth=depth),
        grid_spec=pltpu.PrefetchScalarGridSpec(
            num_scalar_prefetch=1,
            grid=(pieces // GROUP,),
            in_specs=[
                pl.BlockSpec((1, LANES), lambda g, s: (0, 0)),
                pl.BlockSpec((GROUP, wide, wide), lambda g, s: (g, 0, 0)),
                pl.BlockSpec((GROUP, KERNELS, side, side), lambda g, s: (g, 0, 0, 0)),
                pl.BlockSpec((GROUP, side, side), lambda g, s: (g, 0, 0)),
                pl.BlockSpec(columns.shape, lambda g, s: (0, 0)),
                pl.BlockSpec(rows.shape, lambda g, s: (0, 0, 0)),
            ],
            out_specs=pl.BlockSpec((slabs * depth, LANES), lambda g, s: (0, 0)),
        ),
        out_shape=jax.ShapeDtypeStruct((slabs * depth, LANES), jnp.float32),
        compiler_params=pltpu.CompilerParams(vmem_limit_bytes=VMEM_LIMIT),
        name="match_pieces",
    )(lines, code, images, coeffs, inverse_var, jnp.asarray(columns), jnp.asarray(rows))


def binned_sum(chosen, values):
    lanes = values.shape[-1]
    pair = jnp.concatenate(split_pair(values), axis=1)
    sums = jnp.dot(chosen, pair, preferred_element_type=jnp.float32)
    return sums[:, :lanes] + sums[:, lanes:]


def sum_body(slab_ref, out_ref, total_ref, *, depth):
    band, bands = pl.program_id(0), pl.num_programs(0)
    lanes = slab_ref.shape[-1]
    pieces = depth // 2
    holders = slab_ref.shape[0] // depth
    joined = lanes // pieces
    bins_count = total_ref.shape[0]
    patches = bins_count // TILES
    def plane(first):
        return jnp.concatenate(
            [slab_ref[pl.ds(s * depth + first + m, 8), :] for s in range(holders) for m in range(0, pieces, 8)]
        )

    bins = lax.broadcasted_iota(jnp.int32, (bins_count, lanes), 0)
    chosen = []
    for first in range(0, holders, joined):
        code = slab_ref[pl.ds(first * depth + depth - 1, 1), :]
        for s in range(first + 1, first + joined):
            code = code + slab_ref[pl.ds(s * depth + depth - 1, 1), :]
        chosen.append(jnp.where(bins == code.astype(jnp.int32), 1.0, 0.0).astype(jnp.bfloat16))
    chosen = jnp.concatenate(chosen, axis=1)
    numerator = binned_sum(chosen, plane(0))
    denominator = binned_sum(chosen, plane(pieces))
    coadd = numerator / jnp.maximum(denominator, FLOOR)
    out_ref[pl.ds(band * patches, patches), :TILES, :] = coadd.reshape(patches, TILES, lanes)
    term = numerator * coadd

    @pl.when(band == 0)
    def _():
        total_ref[...] = term

    @pl.when(band > 0)
    def _():
        total_ref[...] += term

    @pl.when(band == bands - 1)
    def _():
        total = total_ref[...].reshape(patches, TILES_Y, TILES_X, lanes)
        for target in range(4):
            out_ref[target * patches : (target + 1) * patches, TILES:, :] = total[:, target // 2]


def sum_slabs(slabs, bands, patches, depth):
    devices, lanes = bands * patches, slabs.shape[-1]
    rows = TILES + TILES_X
    return pl.pallas_call(
        functools.partial(sum_body, depth=depth),
        grid=(bands,),
        in_specs=[pl.BlockSpec((slabs.shape[0] // bands, lanes), lambda b: (b, 0))],
        out_specs=pl.BlockSpec((devices, rows, lanes), lambda b: (0, 0, 0)),
        out_shape=jax.ShapeDtypeStruct((devices, rows, lanes), jnp.float32),
        scratch_shapes=[pltpu.VMEM((patches * TILES, lanes), jnp.float32)],
        compiler_params=pltpu.CompilerParams(vmem_limit_bytes=SMALL_LIMIT),
        name="sum_slabs",
    )(slabs)


def place_body(which, part_ref, coadd_ref, detection_ref):
    lanes = part_ref.shape[-1]
    half = lanes // 2
    rows = TILES + TILES_X
    left = lax.broadcasted_iota(jnp.int32, (8, lanes), 1) < half
    for row in range(0, coadd_ref.shape[1], 8):
        for tile in range(rows):
            even = part_ref[pl.ds(2 * row * rows + tile, 8, stride=2 * rows), :]
            odd = part_ref[pl.ds((2 * row + 1) * rows + tile, 8, stride=2 * rows), :]
            upper = jnp.where(left, even, pltpu.roll(odd, half, 1))
            lower = jnp.where(left, pltpu.roll(even, half, 1), odd)
            column = (tile % TILES_X) * lanes
            if tile < TILES:
                top = 2 * (tile // TILES_X)
                coadd_ref[top, row : row + 8, column : column + lanes] = upper
                coadd_ref[top + 1, row : row + 8, column : column + lanes] = lower
            else:
                detection_ref[row : row + 8, column : column + lanes] = jnp.where(
                    which[0] == 0, upper, lower
                )


def place_parts(which, parts, side):
    devices, rows, lanes = parts.shape
    steps = 4
    half = side // 2
    return pl.pallas_call(
        place_body,
        grid_spec=pltpu.PrefetchScalarGridSpec(
            num_scalar_prefetch=1,
            grid=(steps,),
            in_specs=[pl.BlockSpec((devices * rows // steps, lanes), lambda g, s: (g, 0))],
            out_specs=[
                pl.BlockSpec((2 * TILES_Y, half // steps, TILES_X * lanes), lambda g, s: (0, g, 0)),
                pl.BlockSpec((half // steps, TILES_X * lanes), lambda g, s: (g, 0)),
            ],
        ),
        out_shape=[
            jax.ShapeDtypeStruct((2 * TILES_Y, half, TILES_X * lanes), jnp.float32),
            jax.ShapeDtypeStruct((half, TILES_X * lanes), jnp.float32),
        ],
        compiler_params=pltpu.CompilerParams(vmem_limit_bytes=SMALL_LIMIT),
        name="place_parts",
    )(which, parts.reshape(devices * rows, lanes))


def exchange(rows, devices):
    lanes = rows.shape[-1]
    chunks = rows.reshape(devices, -1, 1, lanes)
    return lax.all_to_all(chunks, EVERY, split_axis=0, concat_axis=0, tiled=True).reshape(-1, lanes)


def per_device(images, coeffs, inverse_var, bad_lines, destinations, tile_slots):
    bands, patches = lax.axis_size("band"), lax.axis_size("patch")
    devices = bands * patches
    pieces, side = inverse_var.shape[1:3]
    lines = bad_lines[0].T
    code = (destinations[0, :, 0] * TILES + tile_slots[0]).astype(jnp.float32)
    here = (jnp.arange(LANES) // pieces) == lax.axis_index("patch") % (LANES // pieces)
    code = jnp.where(here, jnp.tile(code, LANES // pieces), 0.0)[None]
    slabs = match_pieces(images[0], coeffs[0], inverse_var[0], lines, code, devices)
    slabs = exchange(slabs, devices)
    parts = sum_slabs(slabs, bands, patches, 2 * pieces + 1)
    parts = lax.all_to_all(parts, EVERY, split_axis=0, concat_axis=0, tiled=True)
    which = jnp.full((1,), lax.axis_index("band") % 2, jnp.int32)
    coadd, detection = place_parts(which, parts, side)
    return (coadd.reshape(1, 1, TILES_Y * side, TILES_X * side), detection[None])


def solution(mesh):
    in_specs = (
        P("band", "patch", None, None),
        P("band", "patch", None, None, None),
        P("band", "patch", None, None),
        P("band", "patch", None),
        P("band", "patch", None),
        P("band", "patch"),
    )
    out_specs = (P("band", "patch", None, None), P("patch", "band", None))
    return jax.shard_map(
        per_device, mesh=mesh, in_specs=in_specs, out_specs=out_specs, check_vma=False
    )
```

time: 133 us -> 118 us (0.89)
  starting transfers between devices: 16 us -> 4.78 us
  Pallas kernels: 26.8 us -> 20.6 us
  blocking collectives: 62.9 us -> 65.4 us
    all_to_all x1 -> x0, starting transfers between devices: 11.5 us -> none  [per_device(): codes = lax.all_to_all(code, EVERY, split_axis=0, concat_axis=0, tiled=True)]
    pallas_call x2, Pallas kernels: 24.8 us -> 18.6 us  [the longest x1 14.4 us: match_pieces(): pl.pallas_call(functools.partial(match_body, depth=depth), grid_spec=pltp...]
    all_to_all x1, blocking collectives: 62.9 us -> 65.4 us  [exchange(): lax.all_to_all(chunks, EVERY, split_axis=0, concat_axis=0, tiled=True)]
  transfers between devices with their start and end apart: 2 -> 1, of which waited for: 1 -> 1; matrix products, arithmetic and copies ran while one was open for 0% -> 0% of each run, Pallas kernels for 14% -> 0%
where the time goes in v2:
time: 118 us; the launch traced here: 117 us
  blocking collectives  65.4 us (55%)
  waiting for transfers between devices  24.7 us (21%)
  Pallas kernels  20.6 us (17%)
  starting transfers between devices  4.78 us (4%)
  other arithmetic  1.2 us (1%)
    all_to_all x1, blocking collectives, exchange(): lax.all_to_all(chunks, EVERY, split_axis=0, concat_axis=0, tiled=True)  65.4 us
    all_to_all x1, waiting for transfers between devices, per_device(): lax.all_to_all(parts, EVERY, split_axis=0, concat_axis=0, tiled=True)  24.7 us
    pallas_call x1, Pallas kernels, match_pieces(): pl.pallas_call(functools.partial(match_body, depth=depth), grid_spec=pltp...  14.4 us
    all_to_all x1, starting transfers between devices, per_device(): lax.all_to_all(parts, EVERY, split_axis=0, concat_axis=0, tiled=True)  4.78 us
    pallas_call x1, Pallas kernels, sum_slabs(): pl.pallas_call(functools.partial(sum_body, depth=depth), grid=(bands,), i...  4.22 us
  transfers between devices with their start and end apart: 1, of which 1 were waited for; matrix products, arithmetic and copies ran while one was open for 0% of the time, Pallas kernels for 0%

profile of v2, /device:TPU:1, one launch (start us, length us, event | category | flops | bytes accessed | tf_op | source)
XLA Modules:
  0.0 117.4 jit_solution(17223489252304716686)
XLA Ops:
  0.6 0.7 fusion.1
  1.3 0.1 tile.13
  1.4 0.5 compare_select_fusion.code_ref
  1.9 14.4 %match_pieces.1 = f32[8320,128]{1,0:T(8,128)} custom-call(s32[2,32]{1,0:T(2,128)} %bitcast.26, f32[1,128]{1,0:T(1,128)} %compare_select_fusion.code_ref, f32[32,168,168]{2,1,0:T(8,128)} %bitcast.23, bf16[32,3,128,128]{3,2,1,0:T(8,128)(2,1)} %bitcast.24, f32[32,128,128]{2,1,0:T(8,128)} %bitcast.25, bf16[504,384]{1,0:T(8,128)(2,1)} %constant.56.clone.columns_ref, ...), custom_call_target="tpu_custom_call" | custom-call | tf_op jit(solution)/shard_map/match_pieces/pallas_call | solution.py:113
  16.3 65.4 %all_to_all.10 = f32[128,65,1,128]{3,2,1,0:T(1,128)S(1)} all-to-all(f32[128,65,1,128]{3,2,1,0:T(1,128)} %bitcast.22), channel_id=1, replica_groups=mesh['band'=4,'patch'=32] {'band','patch'}, dimensions={0} | all-to-all | bytes 8519680 | tf_op jit(solution)/shard_map/all_to_all | solution.py:247
  81.7 4.2 %sum_slabs.1 = f32[128,24,128]{2,1,0:T(8,128)} custom-call(f32[8320,128]{1,0:T(8,128)S(1)} %bitcast.20), custom_call_target="tpu_custom_call" | custom-call | tf_op jit(solution)/shard_map/sum_slabs/pallas_call | solution.py:186
  86.0 4.8 %all-to-all-start.1 = ((f32[128,24,128]{2,1,0:T(8,128)}), f32[128,24,128]{2,1,0:T(8,128)S(1)}, u32[]{:S(2)}, u32[]{:S(2)}) async-start(f32[128,24,128]{2,1,0:T(8,128)} %sum_slabs.1), calls=%async_computation.1 | async-start | bytes 3145728 | tf_op jit(solution)/shard_map/all_to_all | solution.py:261
  90.8 24.7 %all-to-all-done.1 = f32[128,24,128]{2,1,0:T(8,128)S(1)} async-done(((f32[128,24,128]{2,1,0:T(8,128)}), f32[128,24,128]{2,1,0:T(8,128)S(1)}, u32[]{:S(2)}, u32[]{:S(2)}) %all-to-all-start.1) | async-done | bytes 1572896 | tf_op jit(solution)/shard_map/all_to_all | solution.py:261
  115.4 2.0 %place_parts.1 = (f32[4,64,1024]{2,1,0:T(8,128)}, f32[64,1024]{1,0:T(8,128)}) custom-call(s32[1]{0:T(128)} %bitcast.which, f32[3072,128]{1,0:T(8,128)S(1)} %bitcast.21), custom_call_target="tpu_custom_call" | custom-call | tf_op jit(solution)/shard_map/place_parts/pallas_call | solution.py:224
  (1 shorter events, 0.0 us)
Async XLA Ops:
  86.0 29.5 %all-to-all-start.1 = ((f32[128,24,128]{2,1,0:T(8,128)}), f32[128,24,128]{2,1,0:T(8,128)S(1)}, u32[]{:S(2)}, u32[]{:S(2)}) async-start(f32[128,24,128]{2,1,0:T(8,128)} %sum_slabs.1), calls=%async_computation.1 | async-start | bytes 3145728 | tf_op jit(solution)/shard_map/all_to_all | solution.py:261

commit v3 on v2

v3 whole, which is shorter than its diff:
```python
import functools

import jax
import jax.numpy as jnp
import ml_dtypes
import numpy as np
from jax import lax
from jax.experimental import pallas as pl
from jax.experimental.pallas import tpu as pltpu
from jax.sharding import PartitionSpec as P

TILES_X = 8
TILES_Y = 2
TILES = TILES_X * TILES_Y
FRACTIONS = (0.12, 0.25, 0.45)
KERNELS = len(FRACTIONS)
FLOOR = 0.5
EVERY = ("band", "patch")
GROUP = 8
PART_ROWS = TILES + TILES_X // 2
LANES = 128
VMEM_LIMIT = 40 << 20
SMALL_LIMIT = 24 << 20


def split_pair(values):
    high = values.astype(jnp.bfloat16)
    low = (values - high.astype(jnp.float32)).astype(jnp.bfloat16)
    return high, low


def kernel_bands(side, taps):
    offset = np.arange(side + 2 * taps)[None, :] - np.arange(side)[:, None]
    inside = (offset >= 0) & (offset <= 2 * taps)
    reach = np.arange(2 * taps + 1) - taps
    stacked = []
    for fraction in FRACTIONS:
        width = fraction * taps
        total = np.exp(-0.5 * (reach / width) ** 2).sum()
        full = np.where(inside, np.exp(-0.5 * ((offset - taps) / width) ** 2) / total, 0.0)
        full = full.astype(np.float32)
        high = full.astype(ml_dtypes.bfloat16)
        low = (full - high.astype(np.float32)).astype(ml_dtypes.bfloat16)
        stacked.append(np.concatenate([high, low, high], axis=1))
    columns = np.concatenate([matrix.T for matrix in stacked], axis=1)
    rows = np.stack(stacked)
    return columns, rows


def cut_rows(flat, values, start, step):
    side = values.shape[-1]
    half = side // 2
    left = lax.broadcasted_iota(jnp.int32, (8, side), 1) < half
    for row in range(0, half, 8):
        upper = values[row : row + 8]
        lower = values[half + row : half + row + 8]
        first = jnp.where(left, upper, pltpu.roll(lower, half, 1))
        second = jnp.where(left, pltpu.roll(upper, half, 1), lower)
        flat[pl.ds(start + 2 * row * step, 8, stride=2 * step), :] = first
        flat[pl.ds(start + (2 * row + 1) * step, 8, stride=2 * step), :] = second


def weight_of(lines, inverse, piece):
    row_index = lax.broadcasted_iota(jnp.int32, inverse.shape, 0)
    lane_index = lax.broadcasted_iota(jnp.int32, inverse.shape, 1)
    masked = (row_index == lines[0, piece]) | (lane_index == lines[1, piece])
    return jnp.where(masked, 0.0, inverse)


def match_body(
    lines, place, owner_ref, tile_ref, image_ref, coeff_ref, inverse_ref, columns_ref, rows_ref, out_ref, *, depth
):
    side = inverse_ref.shape[-1]
    group = pl.program_id(0)
    pieces = depth // 2

    @pl.when(group == 0)
    def _():
        code = (owner_ref[...] * TILES + tile_ref[...]).astype(jnp.float32)
        code = jnp.concatenate([code] * (LANES // pieces), axis=1)
        part = lax.broadcasted_iota(jnp.int32, code.shape, 1) // pieces
        code = jnp.where(part == lax.rem(place[0], LANES // pieces), code, 0.0)
        code = jnp.broadcast_to(code, (8, LANES))
        for slab in range(0, out_ref.shape[0] // depth, 8):
            out_ref[pl.ds(slab * depth + depth - 1, 8, stride=depth), :] = code

    high, low = split_pair(image_ref[...].reshape(-1, image_ref.shape[-1]))
    stacked = jnp.concatenate([high, high, low], axis=1)
    across_all = jnp.dot(stacked, columns_ref[...], preferred_element_type=jnp.float32)

    def one_pair(pair, carry):
        wide = image_ref.shape[-1]
        across = [across_all[(2 * pair + n) * wide : (2 * pair + n + 1) * wide] for n in range(2)]
        matched = None
        for k in range(KERNELS):
            both = jnp.concatenate([part[:, k * side : (k + 1) * side] for part in across], axis=1)
            high = both.astype(jnp.bfloat16).astype(jnp.float32)
            stacked = jnp.concatenate([high, high, both - high], axis=0).astype(jnp.bfloat16)
            smooth = jnp.dot(rows_ref[k], stacked, preferred_element_type=jnp.float32)
            terms = [
                coeff_ref[2 * pair + n, k].astype(jnp.float32) * smooth[:, n * side : (n + 1) * side]
                for n in range(2)
            ]
            matched = terms if matched is None else [a + b for a, b in zip(matched, terms)]
        for n in range(2):
            p = 2 * pair + n
            piece = group * GROUP + p
            weight = weight_of(lines, inverse_ref[p], piece)
            cut_rows(out_ref, weight * matched[n], piece, depth)
            cut_rows(out_ref, weight, pieces + piece, depth)
        return carry

    for pair in range(GROUP // 2):
        one_pair(pair, 0)


def match_pieces(images, coeffs, inverse_var, lines, place, owners, tiles, slabs):
    pieces, wide = images.shape[0], images.shape[-1]
    side = inverse_var.shape[-1]
    depth = 2 * pieces + 1
    columns, rows = kernel_bands(side, (wide - side) // 2)
    kept = (lines, place, owners, tiles, images, coeffs, inverse_var, jnp.asarray(columns), jnp.asarray(rows))
    kept = [pltpu.with_memory_space_constraint(array, pltpu.HBM) for array in kept]
    return pl.pallas_call(
        functools.partial(match_body, depth=depth),
        grid_spec=pltpu.PrefetchScalarGridSpec(
            num_scalar_prefetch=2,
            grid=(pieces // GROUP,),
            in_specs=[
                pl.BlockSpec((1, pieces), lambda g, *_: (0, 0)),
                pl.BlockSpec((1, pieces), lambda g, *_: (0, 0)),
                pl.BlockSpec((GROUP, wide, wide), lambda g, *_: (g, 0, 0)),
                pl.BlockSpec((GROUP, KERNELS, side, side), lambda g, *_: (g, 0, 0, 0)),
                pl.BlockSpec((GROUP, side, side), lambda g, *_: (g, 0, 0)),
                pl.BlockSpec(columns.shape, lambda g, *_: (0, 0)),
                pl.BlockSpec(rows.shape, lambda g, *_: (0, 0, 0)),
            ],
            out_specs=pl.BlockSpec((slabs * depth, LANES), lambda g, *_: (0, 0)),
        ),
        out_shape=jax.ShapeDtypeStruct((slabs * depth, LANES), jnp.float32),
        compiler_params=pltpu.CompilerParams(vmem_limit_bytes=VMEM_LIMIT),
        name="match_pieces",
    )(*kept)


def binned_sum(chosen, values):
    lanes = values.shape[-1]
    pair = jnp.concatenate(split_pair(values), axis=1)
    sums = jnp.dot(chosen, pair, preferred_element_type=jnp.float32)
    return sums[:, :lanes] + sums[:, lanes:]


def sum_body(slab_ref, out_ref, *, depth, bands):
    lanes = slab_ref.shape[-1]
    half = lanes // 2
    pieces = depth // 2
    holders = slab_ref.shape[0] // (depth * bands)
    joined = lanes // pieces
    patches = out_ref.shape[0] // (PART_ROWS * bands)
    bins = lax.broadcasted_iota(jnp.int32, (patches * TILES, lanes), 0)
    total = None
    for band in range(bands):
        starts = [(band * holders + s) * depth for s in range(holders)]

        def plane(first):
            return jnp.concatenate(
                [slab_ref[start + first + m : start + first + m + 8, :] for start in starts for m in range(0, pieces, 8)]
            )

        chosen = []
        for first in range(0, holders, joined):
            code = sum(slab_ref[start + depth - 1 : start + depth, :] for start in starts[first : first + joined])
            chosen.append(jnp.where(bins == code.astype(jnp.int32), 1.0, 0.0).astype(jnp.bfloat16))
        chosen = jnp.concatenate(chosen, axis=1)
        numerator = binned_sum(chosen, plane(0))
        denominator = binned_sum(chosen, plane(pieces))
        coadd = numerator / jnp.maximum(denominator, FLOOR)
        for patch in range(patches):
            start = (band * patches + patch) * PART_ROWS
            out_ref[start : start + TILES, :] = coadd[patch * TILES : (patch + 1) * TILES]
        term = numerator * coadd
        total = term if total is None else total + term
    left = lax.broadcasted_iota(jnp.int32, (TILES_X, lanes), 1) < half
    for patch in range(patches):
        for top in range(TILES_Y):
            first = (patch * TILES_Y + top) * TILES_X
            tiles = total[first : first + TILES_X]
            later = pltpu.roll(tiles, TILES_X // 2, 0)
            upper = jnp.where(left, tiles, pltpu.roll(later, half, 1))
            lower = jnp.where(left, pltpu.roll(tiles, half, 1), later)
            for low, packed in enumerate((upper, lower)):
                start = ((2 * top + low) * patches + patch) * PART_ROWS + TILES
                out_ref[start : start + TILES_X // 2, :] = packed[: TILES_X // 2]


def sum_slabs(slabs, bands, patches, depth):
    rows, lanes = bands * patches * PART_ROWS, slabs.shape[-1]
    return pl.pallas_call(
        functools.partial(sum_body, depth=depth, bands=bands),
        in_specs=[pl.BlockSpec(memory_space=pltpu.VMEM)],
        out_specs=pl.BlockSpec(memory_space=pltpu.VMEM),
        out_shape=jax.ShapeDtypeStruct((rows, lanes), jnp.float32),
        compiler_params=pltpu.CompilerParams(vmem_limit_bytes=SMALL_LIMIT),
        name="sum_slabs",
    )(slabs)


def place_body(part_ref, coadd_ref, detection_ref):
    lanes = part_ref.shape[-1]
    half = lanes // 2
    left = lax.broadcasted_iota(jnp.int32, (8, lanes), 1) < half

    def column(tile):
        return pl.ds(tile % TILES_X * lanes, lanes)

    for row in range(0, coadd_ref.shape[1], 8):
        for part in range(PART_ROWS):
            even = part_ref[pl.ds(2 * row * PART_ROWS + part, 8, stride=2 * PART_ROWS), :]
            odd = part_ref[pl.ds((2 * row + 1) * PART_ROWS + part, 8, stride=2 * PART_ROWS), :]
            first = jnp.where(left, even, pltpu.roll(odd, half, 1))
            second = jnp.where(left, pltpu.roll(even, half, 1), odd)
            if part < TILES:
                top = 2 * (part // TILES_X)
                coadd_ref[top, row : row + 8, column(part)] = first
                coadd_ref[top + 1, row : row + 8, column(part)] = second
            else:
                detection_ref[row : row + 8, column(part - TILES)] = first
                detection_ref[row : row + 8, column(part - TILES + TILES_X // 2)] = second


def place_parts(parts, side):
    rows, lanes = parts.shape
    steps = 4
    half = side // 2
    return pl.pallas_call(
        place_body,
        grid=(steps,),
        in_specs=[pl.BlockSpec((rows // steps, lanes), lambda g: (g, 0))],
        out_specs=[
            pl.BlockSpec((2 * TILES_Y, half // steps, TILES_X * lanes), lambda g: (0, g, 0)),
            pl.BlockSpec((half // steps, TILES_X * lanes), lambda g: (g, 0)),
        ],
        out_shape=[
            jax.ShapeDtypeStruct((2 * TILES_Y, half, TILES_X * lanes), jnp.float32),
            jax.ShapeDtypeStruct((half, TILES_X * lanes), jnp.float32),
        ],
        compiler_params=pltpu.CompilerParams(vmem_limit_bytes=SMALL_LIMIT),
        name="place_parts",
    )(parts)


def exchange(rows, devices):
    lanes = rows.shape[-1]
    chunks = rows.reshape(devices, -1, 1, lanes)
    return lax.all_to_all(chunks, EVERY, split_axis=0, concat_axis=0, tiled=True).reshape(-1, lanes)


def per_device(images, coeffs, inverse_var, bad_lines, destinations, tile_slots):
    bands, patches = lax.axis_size("band"), lax.axis_size("patch")
    devices = bands * patches
    pieces, side = inverse_var.shape[1:3]
    lines = bad_lines[0].T
    place = jnp.full((1,), lax.axis_index("patch"), jnp.int32)
    owners = destinations[:, :, 0]
    slabs = match_pieces(images[0], coeffs[0], inverse_var[0], lines, place, owners, tile_slots, devices)
    slabs = exchange(slabs, devices)
    parts = sum_slabs(slabs, bands, patches, 2 * pieces + 1)
    coadd, detection = place_parts(exchange(parts, devices), side)
    return (coadd.reshape(1, 1, TILES_Y * side, TILES_X * side), detection[None])


def solution(mesh):
    in_specs = (
        P("band", "patch", None, None),
        P("band", "patch", None, None, None),
        P("band", "patch", None, None),
        P("band", "patch", None),
        P("band", "patch", None),
        P("band", "patch"),
    )
    out_specs = (P("band", "patch", None, None), P("patch", "band", None))
    return jax.shard_map(
        per_device, mesh=mesh, in_specs=in_specs, out_specs=out_specs, check_vma=False
    )
```

time: 118 us -> 106 us (0.90)
  blocking collectives: 65.4 us -> 91.7 us
  waiting for transfers between devices: 24.7 us -> 0 us
  Pallas kernels: 20.6 us -> 13.8 us
  starting transfers between devices: 4.78 us -> 0 us
  other arithmetic: 1.2 us -> 0 us
    all_to_all x1 -> x2, blocking collectives: 65.4 us -> 91.7 us  [exchange(): lax.all_to_all(chunks, EVERY, split_axis=0, concat_axis=0, tiled=True)]
    all_to_all x1 -> x0, waiting for transfers between devices: 24.7 us -> none  [per_device(): lax.all_to_all(parts, EVERY, split_axis=0, concat_axis=0, tiled=True)]
    pallas_call x1, Pallas kernels: 14.4 us -> 9.47 us  [match_pieces(): pl.pallas_call(functools.partial(match_body, depth=depth), grid_spec=pltp...]
    all_to_all x1 -> x0, starting transfers between devices: 4.78 us -> none  [per_device(): lax.all_to_all(parts, EVERY, split_axis=0, concat_axis=0, tiled=True)]
    pallas_call x2, Pallas kernels: 6.21 us -> 4.33 us  [the longest x1 2.42 us: sum_slabs(): pl.pallas_call(functools.partial(sum_body, depth=depth, bands=bands), in_...]
  transfers between devices with their start and end apart: 1 -> 0, of which waited for: 1 -> 0; matrix products, arithmetic and copies ran while one was open for 0% -> 0% of each run, Pallas kernels for 0% -> 0%
where the time goes in v3:
time: 106 us
  blocking collectives  91.7 us (87%)
  Pallas kernels  13.8 us (13%)
    all_to_all x2, blocking collectives, exchange(): lax.all_to_all(chunks, EVERY, split_axis=0, concat_axis=0, tiled=True)  91.7 us
    pallas_call x1, Pallas kernels, match_pieces(): pl.pallas_call(functools.partial(match_body, depth=depth), grid_spec=pltp...  9.47 us
    pallas_call x1, Pallas kernels, sum_slabs(): pl.pallas_call(functools.partial(sum_body, depth=depth, bands=bands), in_...  2.42 us

profile of v3, /device:TPU:1, one launch (start us, length us, event | category | flops | bytes accessed | tf_op | source)
XLA Modules:
  0.0 106.1 jit_solution(6831759069385324869)
XLA Ops:
  0.6 9.5 %match_pieces.1 = f32[8320,128]{1,0:T(8,128)S(1)} custom-call(s32[2,32]{1,0:T(2,128)} %bitcast.21, s32[1]{0:T(128)} %bitcast.2.place, s32[1,32]{1,0:T(1,128)} %bitcast.22, s32[1,32]{1,0:T(1,128)} %tile_ref.1, f32[32,168,168]{2,1,0:T(8,128)} %bitcast.18, bf16[32,3,128,128]{3,2,1,0:T(8,128)(2,1)} %bitcast.19, f32[32,128,128]{2,1,0:T(8,128)} %bitcast.20, ...), custom_call_target="tpu_custom_call" | custom-call | tf_op jit(solution)/shard_map/match_pieces/pallas_call | solution.py:124
  10.1 65.2 %all_to_all.10 = f32[128,65,1,128]{3,2,1,0:T(1,128)S(1)} all-to-all(f32[128,65,1,128]{3,2,1,0:T(1,128)S(1)} %bitcast.15), channel_id=1, replica_groups=mesh['band'=4,'patch'=32] {'band','patch'}, dimensions={0} | all-to-all | bytes 8519680 | tf_op jit(solution)/shard_map/all_to_all | solution.py:255
  75.3 2.4 %sum_slabs.1 = f32[2560,128]{1,0:T(8,128)S(1)} custom-call(f32[8320,128]{1,0:T(8,128)S(1)} %bitcast.14), custom_call_target="tpu_custom_call" | custom-call | tf_op jit(solution)/shard_map/sum_slabs/pallas_call | solution.py:198
  77.7 26.5 %all_to_all.11 = f32[128,20,1,128]{3,2,1,0:T(1,128)S(1)} all-to-all(f32[128,20,1,128]{3,2,1,0:T(1,128)S(1)} %bitcast.17), channel_id=1, replica_groups=mesh['band'=4,'patch'=32] {'band','patch'}, dimensions={0} | all-to-all | bytes 2621440 | tf_op jit(solution)/shard_map/all_to_all | solution.py:255
  104.2 1.9 %place_parts.1 = (f32[4,64,1024]{2,1,0:T(8,128)}, f32[64,1024]{1,0:T(8,128)}) custom-call(f32[2560,128]{1,0:T(8,128)S(1)} %bitcast.16), custom_call_target="tpu_custom_call" | custom-call | tf_op jit(solution)/shard_map/place_parts/pallas_call | solution.py:235

commit v4 on v3

--- a/solution.py
+++ b/solution.py
@@ -213,10 +213,12 @@
     def column(tile):
         return pl.ds(tile % TILES_X * lanes, lanes)
 
+    base = pl.program_id(0) * 2 * coadd_ref.shape[1] * PART_ROWS
     for row in range(0, coadd_ref.shape[1], 8):
         for part in range(PART_ROWS):
-            even = part_ref[pl.ds(2 * row * PART_ROWS + part, 8, stride=2 * PART_ROWS), :]
-            odd = part_ref[pl.ds((2 * row + 1) * PART_ROWS + part, 8, stride=2 * PART_ROWS), :]
+            start = base + 2 * row * PART_ROWS + part
+            even = part_ref[pl.ds(start, 8, stride=2 * PART_ROWS), :]
+            odd = part_ref[pl.ds(start + PART_ROWS, 8, stride=2 * PART_ROWS), :]
             first = jnp.where(left, even, pltpu.roll(odd, half, 1))
             second = jnp.where(left, pltpu.roll(even, half, 1), odd)
             if part < TILES:
@@ -229,13 +231,13 @@
 
 
 def place_parts(parts, side):
-    rows, lanes = parts.shape
+    lanes = parts.shape[-1]
     steps = 4
     half = side // 2
     return pl.pallas_call(
         place_body,
         grid=(steps,),
-        in_specs=[pl.BlockSpec((rows // steps, lanes), lambda g: (g, 0))],
+        in_specs=[pl.BlockSpec(memory_space=pltpu.VMEM)],
         out_specs=[
             pl.BlockSpec((2 * TILES_Y, half // steps, TILES_X * lanes), lambda g: (0, g, 0)),
             pl.BlockSpec((half // steps, TILES_X * lanes), lambda g: (g, 0)),

time: 106 us -> 106 us (level)
  no operation moved by 1% of the time
where the time goes in v4:
time: 106 us
  blocking collectives  91.7 us (87%)
  Pallas kernels  13.8 us (13%)
    all_to_all x2, blocking collectives, exchange(): lax.all_to_all(chunks, EVERY, split_axis=0, concat_axis=0, tiled=True)  91.7 us
    pallas_call x1, Pallas kernels, match_pieces(): pl.pallas_call(functools.partial(match_body, depth=depth), grid_spec=pltp...  9.47 us
    pallas_call x1, Pallas kernels, sum_slabs(): pl.pallas_call(functools.partial(sum_body, depth=depth, bands=bands), in_...  2.42 us

profile of v4, /device:TPU:1, one launch (start us, length us, event | category | flops | bytes accessed | tf_op | source)
XLA Modules:
  0.0 106.1 jit_solution(1295353499755902388)
XLA Ops:
  0.6 9.5 %match_pieces.1 = f32[8320,128]{1,0:T(8,128)S(1)} custom-call(s32[2,32]{1,0:T(2,128)} %bitcast.21, s32[1]{0:T(128)} %bitcast.2.place, s32[1,32]{1,0:T(1,128)} %bitcast.22, s32[1,32]{1,0:T(1,128)} %tile_ref.1, f32[32,168,168]{2,1,0:T(8,128)} %bitcast.18, bf16[32,3,128,128]{3,2,1,0:T(8,128)(2,1)} %bitcast.19, f32[32,128,128]{2,1,0:T(8,128)} %bitcast.20, ...), custom_call_target="tpu_custom_call" | custom-call | tf_op jit(solution)/shard_map/match_pieces/pallas_call | solution.py:124
  10.1 65.2 %all_to_all.10 = f32[128,65,1,128]{3,2,1,0:T(1,128)S(1)} all-to-all(f32[128,65,1,128]{3,2,1,0:T(1,128)S(1)} %bitcast.15), channel_id=1, replica_groups=mesh['band'=4,'patch'=32] {'band','patch'}, dimensions={0} | all-to-all | bytes 8519680 | tf_op jit(solution)/shard_map/all_to_all | solution.py:257
  75.3 2.4 %sum_slabs.1 = f32[2560,128]{1,0:T(8,128)S(1)} custom-call(f32[8320,128]{1,0:T(8,128)S(1)} %bitcast.14), custom_call_target="tpu_custom_call" | custom-call | tf_op jit(solution)/shard_map/sum_slabs/pallas_call | solution.py:198
  77.7 26.5 %all_to_all.11 = f32[128,20,1,128]{3,2,1,0:T(1,128)S(1)} all-to-all(f32[128,20,1,128]{3,2,1,0:T(1,128)S(1)} %bitcast.17), channel_id=1, replica_groups=mesh['band'=4,'patch'=32] {'band','patch'}, dimensions={0} | all-to-all | bytes 2621440 | tf_op jit(solution)/shard_map/all_to_all | solution.py:257
  104.2 1.9 %place_parts.1 = (f32[4,64,1024]{2,1,0:T(8,128)}, f32[64,1024]{1,0:T(8,128)}) custom-call(f32[2560,128]{1,0:T(8,128)S(1)} %bitcast.16), custom_call_target="tpu_custom_call" | custom-call | tf_op jit(solution)/shard_map/place_parts/pallas_call | solution.py:237

commit v5 on v4

--- a/solution.py
+++ b/solution.py
@@ -232,7 +232,7 @@
 
 def place_parts(parts, side):
     lanes = parts.shape[-1]
-    steps = 4
+    steps = 2
     half = side // 2
     return pl.pallas_call(
         place_body,

time: 106 us -> 106 us (level)
  no operation moved by 1% of the time
where the time goes in v5:
time: 106 us
  blocking collectives  91.7 us (87%)
  Pallas kernels  13.2 us (12%)
    all_to_all x2, blocking collectives, exchange(): lax.all_to_all(chunks, EVERY, split_axis=0, concat_axis=0, tiled=True)  91.7 us
    pallas_call x1, Pallas kernels, match_pieces(): pl.pallas_call(functools.partial(match_body, depth=depth), grid_spec=pltp...  9.47 us
    pallas_call x1, Pallas kernels, sum_slabs(): pl.pallas_call(functools.partial(sum_body, depth=depth, bands=bands), in_...  2.42 us

profile of v5, /device:TPU:1, one launch (start us, length us, event | category | flops | bytes accessed | tf_op | source)
XLA Modules:
  0.0 105.6 jit_solution(10179865837894006179)
XLA Ops:
  0.6 9.5 %match_pieces.1 = f32[8320,128]{1,0:T(8,128)S(1)} custom-call(s32[2,32]{1,0:T(2,128)} %bitcast.21, s32[1]{0:T(128)} %bitcast.2.place, s32[1,32]{1,0:T(1,128)} %bitcast.22, s32[1,32]{1,0:T(1,128)} %tile_ref.1, f32[32,168,168]{2,1,0:T(8,128)} %bitcast.18, bf16[32,3,128,128]{3,2,1,0:T(8,128)(2,1)} %bitcast.19, f32[32,128,128]{2,1,0:T(8,128)} %bitcast.20, ...), custom_call_target="tpu_custom_call" | custom-call | tf_op jit(solution)/shard_map/match_pieces/pallas_call | solution.py:124
  10.1 65.2 %all_to_all.10 = f32[128,65,1,128]{3,2,1,0:T(1,128)S(1)} all-to-all(f32[128,65,1,128]{3,2,1,0:T(1,128)S(1)} %bitcast.15), channel_id=1, replica_groups=mesh['band'=4,'patch'=32] {'band','patch'}, dimensions={0} | all-to-all | bytes 8519680 | tf_op jit(solution)/shard_map/all_to_all | solution.py:257
  75.3 2.4 %sum_slabs.1 = f32[2560,128]{1,0:T(8,128)S(1)} custom-call(f32[8320,128]{1,0:T(8,128)S(1)} %bitcast.14), custom_call_target="tpu_custom_call" | custom-call | tf_op jit(solution)/shard_map/sum_slabs/pallas_call | solution.py:198
  77.7 26.5 %all_to_all.11 = f32[128,20,1,128]{3,2,1,0:T(1,128)S(1)} all-to-all(f32[128,20,1,128]{3,2,1,0:T(1,128)S(1)} %bitcast.17), channel_id=1, replica_groups=mesh['band'=4,'patch'=32] {'band','patch'}, dimensions={0} | all-to-all | bytes 2621440 | tf_op jit(solution)/shard_map/all_to_all | solution.py:257
  104.2 1.3 %place_parts.1 = (f32[4,64,1024]{2,1,0:T(8,128)}, f32[64,1024]{1,0:T(8,128)}) custom-call(f32[2560,128]{1,0:T(8,128)S(1)} %bitcast.16), custom_call_target="tpu_custom_call" | custom-call | tf_op jit(solution)/shard_map/place_parts/pallas_call | solution.py:237

commit v6 on v5

--- a/solution.py
+++ b/solution.py
@@ -232,7 +232,7 @@
 
 def place_parts(parts, side):
     lanes = parts.shape[-1]
-    steps = 2
+    steps = 1
     half = side // 2
     return pl.pallas_call(
         place_body,

time: 106 us -> 106 us (level)
  no operation moved by 1% of the time
where the time goes in v6:
time: 106 us
  blocking collectives  91.7 us (87%)
  Pallas kernels  13.3 us (13%)
    all_to_all x2, blocking collectives, exchange(): lax.all_to_all(chunks, EVERY, split_axis=0, concat_axis=0, tiled=True)  91.7 us
    pallas_call x1, Pallas kernels, match_pieces(): pl.pallas_call(functools.partial(match_body, depth=depth), grid_spec=pltp...  9.47 us
    pallas_call x1, Pallas kernels, sum_slabs(): pl.pallas_call(functools.partial(sum_body, depth=depth, bands=bands), in_...  2.42 us

profile of v6, /device:TPU:1, one launch (start us, length us, event | category | flops | bytes accessed | tf_op | source)
XLA Modules:
  0.0 105.7 jit_solution(14120196194372736095)
XLA Ops:
  0.6 9.5 %match_pieces.1 = f32[8320,128]{1,0:T(8,128)S(1)} custom-call(s32[2,32]{1,0:T(2,128)} %bitcast.21, s32[1]{0:T(128)} %bitcast.2.place, s32[1,32]{1,0:T(1,128)} %bitcast.22, s32[1,32]{1,0:T(1,128)} %tile_ref.1, f32[32,168,168]{2,1,0:T(8,128)} %bitcast.18, bf16[32,3,128,128]{3,2,1,0:T(8,128)(2,1)} %bitcast.19, f32[32,128,128]{2,1,0:T(8,128)} %bitcast.20, ...), custom_call_target="tpu_custom_call" | custom-call | tf_op jit(solution)/shard_map/match_pieces/pallas_call | solution.py:124
  10.1 65.2 %all_to_all.10 = f32[128,65,1,128]{3,2,1,0:T(1,128)S(1)} all-to-all(f32[128,65,1,128]{3,2,1,0:T(1,128)S(1)} %bitcast.15), channel_id=1, replica_groups=mesh['band'=4,'patch'=32] {'band','patch'}, dimensions={0} | all-to-all | bytes 8519680 | tf_op jit(solution)/shard_map/all_to_all | solution.py:257
  75.3 2.4 %sum_slabs.1 = f32[2560,128]{1,0:T(8,128)S(1)} custom-call(f32[8320,128]{1,0:T(8,128)S(1)} %bitcast.14), custom_call_target="tpu_custom_call" | custom-call | tf_op jit(solution)/shard_map/sum_slabs/pallas_call | solution.py:198
  77.7 26.5 %all_to_all.11 = f32[128,20,1,128]{3,2,1,0:T(1,128)S(1)} all-to-all(f32[128,20,1,128]{3,2,1,0:T(1,128)S(1)} %bitcast.17), channel_id=1, replica_groups=mesh['band'=4,'patch'=32] {'band','patch'}, dimensions={0} | all-to-all | bytes 2621440 | tf_op jit(solution)/shard_map/all_to_all | solution.py:257
  104.2 1.4 %place_parts.1 = (f32[4,64,1024]{2,1,0:T(8,128)}, f32[64,1024]{1,0:T(8,128)}) custom-call(f32[2560,128]{1,0:T(8,128)S(1)} %bitcast.16), custom_call_target="tpu_custom_call" | custom-call | tf_op jit(solution)/shard_map/place_parts/pallas_call | solution.py:237
